TPU v7x, 32 devices: a whole 2x2x4 slice. The times are simulated.
32 devices in a mesh: pole: 2 (over y), col: 4 (over z), row: 4 (over x, core).
Axes of the slice: x: 2, y: 2, z: 4, core: 2. Of those that a mesh axis runs over, the one named last changes fastest.
Arguments:
- ancestor_inverse: bfloat16 [4, 2048, 2048], P('pole', 'col', 'row'), parts along dimension 0, may hold values from -0.125 to 0.125
- panels: bfloat16 [6, 2048, 512], P('pole', 'col'), parts along dimension 0, may hold values from -0.8984375 to 0.8984375
- block_lists: int32 [6, 16], P('pole'), parts along dimension 0, may hold values from -1 to 15, as said below
- diag_inverse: float32 [6, 256, 512], P('pole', ('col', 'row')), parts along dimension 0, may hold values from -6 to 6
Outputs:
- offdiag: bfloat16 [6, 2048, 512], P('pole', ('col', 'row')), parts along dimension 0
- diag_block: float32 [6, 256, 512], P('pole', ('col', 'row')), parts along dimension 0
There are 2 independent parts, one for each index of `pole`. A program takes and returns all parts, laid end to end along the dimension named above; each array names one. Nothing has to cross between parts.
Inputs may be any that keep to these rules, and one draw needn't show every extreme that they name: `block_lists`: in every supernode, the slots of range r hold distinct blocks of r * 4 to r * 4 + 3, filled slots first and -1 after them; every range has at least one filled slot, and some range has all 4 filled.
All inputs are finite; a program needn't handle non-finite values.
Results may differ from a plain program's by a relative error of at most 0.017.
Values may be sent and summed in bfloat16 or wider, within the bound.
No kernel may reach another device: no remote copies, remote signals or barrier semaphores. Data moves between devices by JAX's collectives and lax.ppermute only.
A program may use at most 64 MiB of HBM per device.

v0:
```python
import jax
import jax.numpy as jnp
from jax import lax
from jax.sharding import PartitionSpec as P

BS = 128
BPR = 4
CAP = 4


def from_root(value, axis, source):
    kept = jnp.where(lax.axis_index(axis) == source, value, 0).astype(value.dtype)
    return lax.psum(kept, axis)


def complex_product(first, second):
    half = first.shape[1] // 2
    return jnp.concatenate(
        [first[:, :half] - second[:, half:], first[:, half:] + second[:, :half]], axis=1
    )


def on_device(ancestor_inverse, panels, block_lists, diag_inverse):
    here_col = lax.axis_index("col")
    here_row = lax.axis_index("row")
    nsup = panels.shape[0]
    width = panels.shape[2] // 2
    mine = lax.dynamic_slice_in_dim(block_lists, here_col * CAP, CAP, 1)
    theirs = lax.dynamic_slice_in_dim(block_lists, here_row * CAP, CAP, 1)
    row_mask = jnp.repeat((mine >= 0).astype(jnp.bfloat16), BS, axis=1)
    masked = panels * row_mask[:, :, None]
    blocks = ancestor_inverse.reshape(2, BPR, BS, BPR, BS)
    pieces = []
    for k in range(nsup):
        range_rows = from_root(masked[k], "col", here_row)
        row_offset = jnp.clip(mine[k] - here_col * BPR, 0, BPR - 1)
        col_offset = jnp.clip(theirs[k] - here_row * BPR, 0, BPR - 1)
        picked = jnp.take(blocks, row_offset, axis=1)
        picked = jnp.take(picked, col_offset, axis=3).reshape(2, CAP * BS, CAP * BS)
        product_first = jnp.dot(picked[0], range_rows, preferred_element_type=jnp.float32)
        product_second = jnp.dot(picked[1], range_rows, preferred_element_type=jnp.float32)
        pieces.append(
            lax.psum_scatter(
                (
                    complex_product(product_first, product_second)
                    * row_mask[k][:, None].astype(jnp.float32)
                ).astype(jnp.bfloat16),
                "row",
                scatter_dimension=0,
                tiled=True,
            ).astype(jnp.float32)
        )
    summed = jnp.stack(pieces)
    offdiag = (-summed).astype(jnp.bfloat16)
    share = summed.shape[1]
    own_rows = lax.dynamic_slice_in_dim(masked, here_row * share, share, 1)
    dims = (((0,), (0,)), ((), ()))
    updates = []
    for k in range(nsup):
        first = lax.dot_general(
            own_rows[k][:, :width], offdiag[k], dims, preferred_element_type=jnp.float32
        )
        second = lax.dot_general(
            own_rows[k][:, width:], offdiag[k], dims, preferred_element_type=jnp.float32
        )
        updates.append(complex_product(first, second))
    updates = jnp.stack(updates)
    own_update = lax.psum_scatter(updates, ("col", "row"), scatter_dimension=1, tiled=True)
    return (offdiag, diag_inverse - own_update)


def solution(mesh):
    return jax.shard_map(
        on_device,
        mesh=mesh,
        in_specs=(
            P("pole", "col", "row"),
            P("pole", "col", None),
            P("pole", None),
            P("pole", ("col", "row"), None),
        ),
        out_specs=(P("pole", ("col", "row"), None), P("pole", ("col", "row"), None)),
        check_vma=False,
    )
```

profile of v0, /device:TPU:0, one launch (start us, length us, event | category | flops | bytes accessed | tf_op | source)
XLA Modules:
  0.0 227.8 jit_solution(14445422382365033342)
XLA Ops:
  7.2 0.8 compare_convert_fusion
  8.1 1.7 broadcast_multiply_fusion
  9.7 1.2 fusion.23
  11.0 0.6 copy-done.9
  11.8 0.4 copy-done.7
  12.2 1.1 reshape.115
  13.3 1.5 copy.31
  14.8 1.7 gather_fusion.4
  16.5 1.4 select_bitcast_fusion.1
  17.9 1.1 copy.40
  19.0 2.9 %gather_fusion.5 = bf16[4,2,4,128,128]{4,3,2,1,0:T(8,128)(2,1)} fusion(bf16[2,4,128,4,128]{4,2,3,1,0:T(8,128)(2,1)} %copy.40, s32[1024]{0:T(1024)S(1)} %pad_clamp_fusion), kind=kCustom, calls=%fused_computation.5.clone | custom fusion | bytes 2097168 | tf_op jit(solution)/shard_map/jit(_take)/gather | solution.py:39
  21.9 1.4 select_bitcast_fusion
  23.4 1.2 copy.41
  24.6 1.2 copy.42
  25.8 1.7 gather_fusion.2
  27.5 1.6 gather_fusion
  29.1 1.4 select_bitcast_fusion.3
  30.5 1.1 copy.36
  31.6 0.5 copy-done
  32.3 1.0 copy.32
  33.3 2.0 gather_fusion.1
  35.5 0.9 fusion.36
  36.3 0.4 copy.33
  36.8 2.0 gather_fusion.3
  39.0 1.2 copy.37
  40.3 1.2 copy.38
  41.5 0.4 copy.34
  42.0 40.9 %all-reduce.3.cloned.1.call-done = (bf16[512,512]{1,0:T(8,128)(2,1)}, bf16[512,512]{1,0:T(8,128)(2,1)}, bf16[512,512]{1,0:T(8,128)(2,1)}) async-done(((bf16[512,512]{1,0:T(8,128)(2,1)}, bf16[512,512]{1,0:T(8,128)(2,1)}, bf16[512,512]{1,0:T(8,128)(2,1)}), (bf16[512,512]{1,0:T(8,128)(2,1)}, bf16[512,512]{1,0:T(8,128)(2,1)}, bf16[512,512]{1,0:T(8,128)(2,1)})) %all-reduce.3.cloned.1.call-update) | async-done | bytes 1572880 | tf_op jit(solution)/shard_map/psum | solution.py:13
  82.9 1.7 fusion.3
  84.7 0.5 fusion.6
  85.5 1.0 copy.48
  86.6 1.8 fusion.9
  88.4 0.5 fusion.12
  89.2 1.0 copy.46
  90.3 1.6 fusion.15
  92.0 0.5 fusion.18
  92.8 1.0 copy.44
  94.0 13.5 %reduce-scatter.17.cloned.1.call-done = bf16[128,512]{1,0:T(8,128)(2,1)} async-done(((bf16[512,512]{1,0:T(8,128)(2,1)}), bf16[128,512]{1,0:T(8,128)(2,1)}) %reduce-scatter.17.cloned.1.call-update) | async-done | bytes 131088
  107.5 1.0 copy.49
  108.5 23.2 %reduce-scatter.15.cloned.1.call-done = bf16[128,512]{1,0:T(8,128)(2,1)} async-done(((bf16[512,512]{1,0:T(8,128)(2,1)}), bf16[128,512]{1,0:T(8,128)(2,1)}) %reduce-scatter.15.cloned.1.call-update) | async-done | bytes 131088
  131.7 1.0 copy.47
  132.7 23.0 %reduce-scatter.13.cloned.1.call-done = bf16[128,512]{1,0:T(8,128)(2,1)} async-done(((bf16[512,512]{1,0:T(8,128)(2,1)}), bf16[128,512]{1,0:T(8,128)(2,1)}) %reduce-scatter.13.cloned.1.call-update) | async-done | bytes 131088
  155.7 1.0 copy.45
  157.3 0.2 fusion.26
  158.7 1.3 pad_maximum_fusion
  160.1 0.9 copy.43
  161.0 58.7 %reduce-scatter.11.cloned.1.call-done = f32[3,16,512]{2,1,0:T(8,128)} async-done(((f32[3,256,512]{2,1,0:T(8,128)}), f32[3,16,512]{2,1,0:T(8,128)}) %reduce-scatter.11.cloned.1.call-update) | async-done | bytes 98320 | tf_op jit(solution)/shard_map/reduce_scatter | solution.py:68
  219.7 1.5 sub.69
  (64 shorter events, 4.1 us)
Async XLA Ops:
  7.2 75.8 %all-reduce.3.cloned.1.call-start = ((), (), s32[]{:S(2)}) async-start(), calls=%async_computation.8 | async-start | bytes 3145728 | tf_op jit(solution)/shard_map/psum | solution.py:13
  10.9 0.7 copy-start.9
  11.0 1.2 copy-start.7
  11.0 96.5 %reduce-scatter.17.cloned.1.call-start = ((), (), s32[]{:S(2)}) async-start(), calls=%async_computation.7 | async-start | bytes 655360
  30.5 1.6 copy-start
  39.0 2.4 %copy-start.3 = (bf16[1,4,128,4,128]{4,2,1,0,3:T(8,128)(2,1)S(1)}, bf16[1,4,128,4,128]{4,2,1,0,3:T(8,128)(2,1)}, u32[]{:S(2)}) copy-start(bf16[1,4,128,4,128]{4,2,1,0,3:T(8,128)(2,1)} %get-tuple-element.50) | copy-start | bytes 1572868
  41.5 43.2 %copy-start.1 = (bf16[1,4,128,4,128]{4,3,2,1,0:T(4,128)(2,1)S(1)}, bf16[1,4,128,4,128]{4,3,2,1,0:T(4,128)(2,1)}, u32[]{:S(2)}) copy-start(bf16[1,4,128,4,128]{4,3,2,1,0:T(4,128)(2,1)} %copy.41) | copy-start | bytes 1572868
  82.9 1.8 copy-start.6
  86.5 1.9 copy-start.2
  86.6 45.1 %reduce-scatter.15.cloned.1.call-start = ((), (), s32[]{:S(2)}) async-start(), calls=%async_computation.6 | async-start | bytes 655360
  86.6 1.8 copy-start.5
  90.3 1.7 copy-start.4
  90.3 65.4 %reduce-scatter.13.cloned.1.call-start = ((), (), s32[]{:S(2)}) async-start(), calls=%async_computation.5 | async-start | bytes 655360
  93.9 125.8 %reduce-scatter.11.cloned.1.call-start = ((), (), s32[]{:S(2)}) async-start(), calls=%async_computation.4 | async-start | bytes 1671168 | tf_op jit(solution)/shard_map/reduce_scatter | solution.py:68
  160.1 59.6 %copy-start.8 = (f32[3,16,512]{2,1,0:T(8,128)S(1)}, f32[3,16,512]{2,1,0:T(8,128)}, u32[]{:S(2)}) copy-start(f32[3,16,512]{2,1,0:T(8,128)} %param.11) | copy-start | bytes 294916
Sparse Core Ops, SparseCore 0:
  11.1 71.7 all-reduce.2
  86.7 20.7 reduce-scatter.16
  110.0 21.6 reduce-scatter.14
  134.0 21.6 reduce-scatter.12
  160.2 59.4 reduce-scatter.10
where the time goes:
time: 228 us
  waiting for transfers between devices  159 us (70%)
  local copies, waits for them, and re-layouts  33.3 us (15%)
  between operations  14.2 us (6%)
  other arithmetic  12.7 us (6%)
  matrix products  8.05 us (4%)
    unnamed x8, waiting for transfers between devices  59.8 us
    reduce_scatter x1, waiting for transfers between devices, on_device(): lax.psum_scatter(updates, ('col', 'row'), scatter_dimension=1, tiled=True)  58.7 us
    psum x1, waiting for transfers between devices, from_root(): return lax.psum(kept, axis)  40.9 us
    unnamed x29, local copies, waits for them, and re-layouts  8.66 us
    gather x3, local copies, waits for them, and re-layouts, on_device(): picked = jnp.take(picked, col_offset, axis=3).reshape(2, CAP * BS, CAP * BS)  6.85 us
    dot_general x3, matrix products, on_device(): jnp.dot(picked[1], range_rows, preferred_element_type=jnp.float32)  5.12 us
    gather x3, local copies, waits for them, and re-layouts, on_device(): picked = jnp.take(blocks, row_offset, axis=1)  5.01 us
  transfers between devices with their start and end apart: 5, of which 5 were waited for; matrix products, arithmetic and copies ran while one was open for 17% of the time, Pallas kernels for 0%

commit v1 on v0

--- a/solution.py
+++ b/solution.py
@@ -8,9 +8,14 @@
 CAP = 4
 
 
+def _trace_run(shard_in, shard_axis):
+    arr_now = jnp.sum(lax.all_gather(shard_in, shard_axis), axis=0)
+    return arr_now
+
+
 def from_root(value, axis, source):
     kept = jnp.where(lax.axis_index(axis) == source, value, 0).astype(value.dtype)
-    return lax.psum(kept, axis)
+    return _trace_run(kept, axis)
 
 
 def complex_product(first, second):

time: 228 us -> 296 us (1.30)
  waiting for transfers between devices: 159 us -> 218 us
  other arithmetic: 12.7 us -> 22.8 us
    all_gather x0 -> x3, waiting for transfers between devices: none -> 94.1 us  [_trace_run(): arr_now = jnp.sum(lax.all_gather(shard_in, shard_axis), axis=0)]
    psum x1 -> x0, waiting for transfers between devices: 40.9 us -> none  [from_root(): return lax.psum(kept, axis)]
    reduce_sum x0 -> x3, other arithmetic: none -> 6.53 us  [_trace_run(): arr_now = jnp.sum(lax.all_gather(shard_in, shard_axis), axis=0)]
    unnamed x8 -> x10, waiting for transfers between devices: 59.8 us -> 65.6 us
    unnamed x29 -> x21, local copies, waits for them, and re-layouts: 8.66 us -> 7.27 us
  transfers between devices with their start and end apart: 5 -> 7, of which waited for: 5 -> 7; matrix products, arithmetic and copies ran while one was open for 17% -> 18% of each run, Pallas kernels for 0% -> 0%
where the time goes in v1:
time: 296 us; the launch traced here: 295 us
  waiting for transfers between devices  218 us (74%)
  local copies, waits for them, and re-layouts  32.3 us (11%)
  other arithmetic  22.8 us (8%)
  between operations  14.5 us (5%)
  matrix products  6.58 us (2%)
    all_gather x3, waiting for transfers between devices, _trace_run(): arr_now = jnp.sum(lax.all_gather(shard_in, shard_axis), axis=0)  94.1 us
    unnamed x10, waiting for transfers between devices  65.6 us
    reduce_scatter x1, waiting for transfers between devices, on_device(): lax.psum_scatter(updates, ('col', 'row'), scatter_dimension=1, tiled=True)  58.7 us
    gather x3, local copies, waits for them, and re-layouts, on_device(): picked = jnp.take(picked, col_offset, axis=3).reshape(2, CAP * BS, CAP * BS)  7.91 us
    unnamed x21, local copies, waits for them, and re-layouts  7.27 us
    reduce_sum x3, other arithmetic, _trace_run(): arr_now = jnp.sum(lax.all_gather(shard_in, shard_axis), axis=0)  6.53 us
  transfers between devices with their start and end apart: 7, of which 7 were waited for; matrix products, arithmetic and copies ran while one was open for 18% of the time, Pallas kernels for 0%

profile of v1, /device:TPU:0, one launch (start us, length us, event | category | flops | bytes accessed | tf_op | source)
XLA Modules:
  0.0 295.0 jit_solution(6540092812411950276)
XLA Ops:
  7.2 0.8 compare_convert_fusion
  8.1 1.7 broadcast_multiply_fusion
  9.7 1.2 slice_select_fusion.2
  11.0 0.7 all-gather.6.cloned.1.call-update
  11.8 0.7 all-gather.4.cloned.1.call-update
  12.5 1.1 reshape.106
  13.6 1.5 copy.31
  15.3 1.7 gather_fusion.4
  16.9 1.4 select_bitcast_fusion.1
  18.3 1.1 copy.40
  19.4 1.7 gather_fusion.2
  21.1 1.4 select_bitcast_fusion.3
  22.5 1.1 copy.36
  23.6 3.0 %gather_fusion.5 = bf16[4,2,4,128,128]{4,3,2,1,0:T(8,128)(2,1)} fusion(bf16[2,4,128,4,128]{4,2,3,1,0:T(8,128)(2,1)} %copy.40, s32[1024]{0:T(1024)S(1)} %pad_clamp_fusion), kind=kCustom, calls=%fused_computation.5.clone | custom fusion | bytes 2097168 | tf_op jit(solution)/shard_map/jit(_take)/gather | solution.py:44
  26.6 2.5 select_bitcast_fusion
  29.0 3.0 %gather_fusion.3 = bf16[4,2,4,128,128]{4,3,2,1,0:T(8,128)(2,1)} fusion(bf16[2,4,128,4,128]{4,2,3,1,0:T(8,128)(2,1)} %copy.36, s32[1024]{0:T(1024)S(1)} %pad_clamp_fusion.2), kind=kCustom, calls=%fused_computation.4.clone | custom fusion | bytes 2097168 | tf_op jit(solution)/shard_map/jit(_take)/gather | solution.py:44
  32.0 1.5 select_bitcast_fusion.2
  33.7 1.3 copy.42
  34.9 1.2 copy.41
  36.3 1.2 copy.38
  37.5 1.2 copy.37
  38.7 1.7 gather_fusion
  40.4 1.4 select_bitcast_fusion.5
  41.8 1.1 copy.32
  42.8 2.0 gather_fusion.1
  46.1 13.4 %all-gather.8.cloned.1.call-done = bf16[4,512,512]{2,1,0:T(8,128)(2,1)} async-done(((bf16[1,512,512]{2,1,0:T(8,128)(2,1)}), bf16[4,512,512]{2,1,0:T(8,128)(2,1)}) %all-gather.8.cloned.1.call-update) | async-done | bytes 2097168 | tf_op jit(solution)/shard_map/all_gather | solution.py:12
  59.5 2.2 reduce_sum.38
  61.7 1.6 fusion.3
  63.3 0.5 fusion.6
  64.1 1.1 copy.48
  65.3 40.3 %all-gather.6.cloned.1.call-done = bf16[4,512,512]{2,1,0:T(8,128)(2,1)} async-done(((bf16[1,512,512]{2,1,0:T(8,128)(2,1)}), bf16[4,512,512]{2,1,0:T(8,128)(2,1)}) %all-gather.6.cloned.1.call-update) | async-done | bytes 2097168 | tf_op jit(solution)/shard_map/all_gather | solution.py:12
  105.6 2.2 reduce_sum.37
  107.8 1.6 fusion.9
  109.4 0.5 fusion.12
  110.2 1.0 copy.46
  111.3 40.3 %all-gather.4.cloned.1.call-done = bf16[4,512,512]{2,1,0:T(8,128)(2,1)} async-done(((bf16[1,512,512]{2,1,0:T(8,128)(2,1)}), bf16[4,512,512]{2,1,0:T(8,128)(2,1)}) %all-gather.4.cloned.1.call-update) | async-done | bytes 2097168 | tf_op jit(solution)/shard_map/all_gather | solution.py:12
  151.6 2.2 reduce_sum.36
  155.1 1.0 copy.44
  156.3 18.2 %reduce-scatter.17.cloned.1.call-done = bf16[128,512]{1,0:T(8,128)(2,1)} async-done(((bf16[512,512]{1,0:T(8,128)(2,1)}), bf16[128,512]{1,0:T(8,128)(2,1)}) %reduce-scatter.17.cloned.1.call-update) | async-done | bytes 131088
  174.5 1.0 copy.49
  175.5 23.0 %reduce-scatter.15.cloned.1.call-done = bf16[128,512]{1,0:T(8,128)(2,1)} async-done(((bf16[512,512]{1,0:T(8,128)(2,1)}), bf16[128,512]{1,0:T(8,128)(2,1)}) %reduce-scatter.15.cloned.1.call-update) | async-done | bytes 131088
  198.5 1.0 copy.47
  199.5 23.0 %reduce-scatter.13.cloned.1.call-done = bf16[128,512]{1,0:T(8,128)(2,1)} async-done(((bf16[512,512]{1,0:T(8,128)(2,1)}), bf16[128,512]{1,0:T(8,128)(2,1)}) %reduce-scatter.13.cloned.1.call-update) | async-done | bytes 131088
  222.5 1.0 copy.45
  225.5 1.3 pad_maximum_fusion
  226.9 0.9 copy.43
  227.8 58.7 %reduce-scatter.11.cloned.1.call-done = f32[3,16,512]{2,1,0:T(8,128)} async-done(((f32[3,256,512]{2,1,0:T(8,128)}), f32[3,16,512]{2,1,0:T(8,128)}) %reduce-scatter.11.cloned.1.call-update) | async-done | bytes 98320 | tf_op jit(solution)/shard_map/reduce_scatter | solution.py:73
  286.6 1.5 sub.69
  (65 shorter events, 6.0 us)
Async XLA Ops:
  7.2 52.3 %all-gather.8.cloned.1.call-start = ((), (), s32[]{:S(2)}) async-start(), calls=%async_computation.6 | async-start | bytes 2621440 | tf_op jit(solution)/shard_map/all_gather | solution.py:12
  10.9 1.6 copy-start.3
  11.0 94.6 %all-gather.6.cloned.1.call-start = ((), (), s32[]{:S(2)}) async-start(), calls=%async_computation.5 | async-start | bytes 2621440 | tf_op jit(solution)/shard_map/all_gather | solution.py:12
  11.7 139.9 %all-gather.4.cloned.1.call-start = ((), (), s32[]{:S(2)}) async-start(), calls=%async_computation.4 | async-start | bytes 2621440 | tf_op jit(solution)/shard_map/all_gather | solution.py:12
  12.5 162.0 %reduce-scatter.17.cloned.1.call-start = ((), (), s32[]{:S(2)}) async-start(), calls=%async_computation.10 | async-start | bytes 655360
  13.6 1.5 copy-start.5
  32.0 1.6 copy-start
  61.7 1.6 copy-start.2
  65.2 133.3 %reduce-scatter.15.cloned.1.call-start = ((), (), s32[]{:S(2)}) async-start(), calls=%async_computation.9 | async-start | bytes 655360
  107.7 1.6 copy-start.1
  111.2 111.3 %reduce-scatter.13.cloned.1.call-start = ((), (), s32[]{:S(2)}) async-start(), calls=%async_computation.8 | async-start | bytes 655360
  156.2 130.4 %reduce-scatter.11.cloned.1.call-start = ((), (), s32[]{:S(2)}) async-start(), calls=%async_computation.7 | async-start | bytes 1671168 | tf_op jit(solution)/shard_map/reduce_scatter | solution.py:73
  226.9 59.7 %copy-start.4 = (f32[3,16,512]{2,1,0:T(8,128)S(1)}, f32[3,16,512]{2,1,0:T(8,128)}, u32[]{:S(2)}) copy-start(f32[3,16,512]{2,1,0:T(8,128)} %param.11) | copy-start | bytes 294916
Sparse Core Ops, SparseCore 0:
  11.1 48.3 all-gather.7
  61.1 44.4 all-gather.5
  107.1 44.4 all-gather.3
  154.0 20.4 reduce-scatter.16
  176.8 21.6 reduce-scatter.14
  200.8 21.6 reduce-scatter.12
  227.0 59.5 reduce-scatter.10
